TPU v7x, 256 devices: a whole 4x4x8 slice. The times are simulated.
256 devices in a mesh: gx: 8 (over y, core), gy: 32 (over z, x).
Axes of the slice: x: 4, y: 4, z: 8, core: 2. Of those that a mesh axis runs over, the one named last changes fastest.
Arguments:
- state_mean: float32 [2, 512, 1024], P(None, 'gy', 'gx'), may hold values from -6 to 6
- state_spread: bfloat16 [2, 512, 1024, 128], P(None, 'gy', 'gx'), may hold values from -6 to 6
- obs_value: float32 [2, 8, 32, 4], replicated, may hold values from -8 to 8
- obs_var: float32 [2, 8, 32, 4], replicated, may hold values from 0.25 to 4
- obs_col: int32 [2, 8, 32, 4], replicated, may hold values from 0 to 127
- obs_row: int32 [2, 8, 32, 4], replicated, may hold values from 0 to 15
- obs_level: int32 [2, 8, 32, 4], replicated, may hold values from 0 to 1
Outputs:
- analysis_mean: float32 [2, 512, 1024], P(None, 'gy', 'gx')
- analysis_spread: bfloat16 [2, 512, 1024, 128], P(None, 'gy', 'gx')
All inputs are finite; a program needn't handle non-finite values.
Results may differ from a plain program's by a relative error of at most 0.011.
Values may be sent and summed in bfloat16 or wider, within the bound.
A program may use at most 64 MiB of HBM per device.

v0:
```python
import jax
import jax.numpy as jnp
from jax import lax
from jax.sharding import PartitionSpec as P

PRECISE = lax.Precision.HIGHEST


def taper(dist_sq, radius):
    ratio = jnp.sqrt(dist_sq) / radius
    ratio_safe = jnp.maximum(ratio, 1.0)
    inner_part = (((-0.25 * ratio + 0.5) * ratio + 0.625) * ratio - 5.0 / 3.0) * ratio * ratio + 1.0
    outer_part = (
        ((((ratio / 12.0 - 0.5) * ratio + 0.625) * ratio + 5.0 / 3.0) * ratio - 5.0) * ratio
        + 4.0
        - 2.0 / (3.0 * ratio_safe)
    )
    return jnp.where(ratio <= 1.0, inner_part, jnp.where(ratio < 2.0, outer_part, 0.0))


def add_panel(totals, panel, obs_x, obs_y, spread_rows, row_y, col_x, radius):
    panel_zb, panel_qb, panel_eb = panel
    members = spread_rows.shape[2]
    delta_x = (col_x[:, None] - obs_x[None, :]).astype(jnp.float32)
    delta_y = (row_y[:, None] - obs_y[None, :]).astype(jnp.float32)
    taper_vals = taper(delta_x * delta_x + delta_y * delta_y, radius)

    def per_level(operands):
        spread_lev, mean_inc, spread_inc = operands
        covariance = jnp.dot(spread_lev, panel_zb.T, preferred_element_type=jnp.float32) / (
            members - 1.0
        )
        gain_bf = (taper_vals * covariance).astype(jnp.bfloat16)
        mean_inc = mean_inc + jnp.dot(gain_bf, panel_eb, preferred_element_type=jnp.float32)
        spread_inc = spread_inc + jnp.dot(gain_bf, panel_qb, preferred_element_type=jnp.float32)
        return (mean_inc, spread_inc)

    return lax.map(per_level, (spread_rows, totals[0], totals[1]))


def body(state_mean, state_spread, obs_value, obs_var, obs_col, obs_row, obs_level):
    levels, rows_y, cols_x, members = state_spread.shape
    count_x = lax.axis_size("gx")
    count_y = lax.axis_size("gy")
    radius = count_x * cols_x // 2
    at_x = lax.axis_index("gx")
    at_y = lax.axis_index("gy")
    blocks = obs_value.shape[0]
    root_dof = jnp.sqrt(jnp.float32(members - 1))
    identity = jnp.eye(members, dtype=jnp.float32)
    cell_count = rows_y * cols_x
    cell_ids = jnp.arange(cell_count, dtype=jnp.int32)
    row_y = at_y * rows_y + cell_ids // cols_x
    col_x = at_x * cols_x + cell_ids % cols_x
    mean_now = state_mean.reshape(levels, cell_count)
    spread = state_spread.reshape(levels, cell_count, members)
    for block_idx in range(blocks):
        loc_x = obs_col[block_idx][at_x, at_y]
        loc_y = obs_row[block_idx][at_x, at_y]
        loc_lev = obs_level[block_idx][at_x, at_y]
        flat_cell = loc_y * cols_x + loc_x
        prior_obs = mean_now[loc_lev, flat_cell]
        panel_z = spread[loc_lev, flat_cell, :].astype(jnp.float32)
        obs_sd = jnp.sqrt(obs_var[block_idx][at_x, at_y])
        weighted = panel_z / (obs_sd[:, None] * root_dof)
        innov_norm = (obs_value[block_idx][at_x, at_y] - prior_obs) / obs_sd
        zeros_init = (
            jnp.zeros((levels, cell_count), jnp.float32),
            jnp.zeros((levels, cell_count, members), jnp.float32),
        )
        all_x = (
            jnp.arange(count_x, dtype=jnp.int32)[:, None, None] * cols_x + obs_col[block_idx]
        ).reshape(-1)
        all_y = (
            jnp.arange(count_y, dtype=jnp.int32)[None, :, None] * rows_y + obs_row[block_idx]
        ).reshape(-1)
        gram_term = jnp.dot(weighted.T, weighted, precision=PRECISE)
        proj_term = jnp.dot(weighted.T, innov_norm, precision=PRECISE)
        gram_all, proj_all = lax.psum((gram_term, proj_term), ("gx", "gy"))
        factor = jnp.linalg.cholesky(identity + gram_all)
        ens_weights = jax.scipy.linalg.cho_solve((factor, True), proj_all)
        panel_e = (innov_norm - jnp.dot(weighted, ens_weights, precision=PRECISE)) / obs_sd
        solved = jax.scipy.linalg.cho_solve((factor, True), weighted.T)
        panel_q = (root_dof / obs_sd)[:, None] * solved.T
        panel_zb = panel_z.astype(jnp.bfloat16)
        panel_qb = panel_q.astype(jnp.bfloat16)
        panel_eb = panel_e.astype(jnp.bfloat16)
        totals = add_panel(
            zeros_init,
            (
                lax.all_gather(panel_zb, ("gx", "gy"), axis=0, tiled=True),
                lax.all_gather(panel_qb, ("gx", "gy"), axis=0, tiled=True),
                lax.all_gather(panel_eb, ("gx", "gy"), axis=0, tiled=True),
            ),
            all_x,
            all_y,
            spread,
            row_y,
            col_x,
            radius,
        )
        mean_now = mean_now + totals[0]
        spread = (spread.astype(jnp.float32) - 0.5 * totals[1]).astype(jnp.bfloat16)
    return (
        mean_now.reshape(levels, rows_y, cols_x),
        spread.reshape(levels, rows_y, cols_x, members),
    )


def solution(mesh):
    return jax.shard_map(
        body,
        mesh=mesh,
        in_specs=(P(None, "gy", "gx"), P(None, "gy", "gx", None), P(), P(), P(), P(), P()),
        out_specs=(P(None, "gy", "gx"), P(None, "gy", "gx", None)),
        check_vma=False,
    )
```

profile of v0, /device:TPU:1, one launch (start us, length us, event | category | flops | bytes accessed | tf_op | source)
XLA Modules:
  0.0 903.8 jit_solution(16388274281650954638)
XLA Ops:
  7.2 0.7 fusion.89
  8.0 0.7 fusion.90
  8.7 0.7 fusion.88
  9.4 0.7 fusion.87
  10.6 1.4 gather_fusion
  12.0 1.0 fusion.84
  13.3 0.7 copy.38
  14.0 0.6 gather_fusion.1
  14.7 0.7 fusion.86
  15.4 66.7 %all-gather = bf16[256,4,128]{2,1,0:T(4,128)(2,1)S(1)} all-gather(bf16[1,4,128]{2,1,0:T(4,128)(2,1)S(1)} %bitcast.216), channel_id=1, replica_groups=mesh['gx'=8,'gy'=32] {'gx','gy'}, dimensions={0}, use_global_device_ids=true | all-gather | bytes 263168 | tf_op jit(solution)/shard_map/all_gather | solution.py:91
  83.5 0.7 multiply_reduce_fusion
  84.2 0.5 broadcast_multiply_fusion
  84.9 0.5 fusion.81
  85.5 0.6 fusion.91
  86.1 0.7 fusion.62
  86.8 75.3 %psum.29 = f32[128]{0:T(128)S(1)} all-reduce(f32[128]{0:T(128)S(1)} %convolution_bitcast_fusion.9), channel_id=1, replica_groups=mesh['gx'=8,'gy'=32] {'gx','gy'}, use_global_device_ids=true, to_apply=%region_3.5 | all-reduce | flops 128 | bytes 1024 | tf_op jit(solution)/shard_map/psum | solution.py:79
  162.1 98.1 %all-reduce.5.cloned.1.call-done = f32[128,128]{0,1:T(8,128)} async-done(((f32[128,128]{0,1:T(8,128)}), f32[128,128]{0,1:T(8,128)}) %all-reduce.5.cloned.1.call-update) | async-done | bytes 65552 | tf_op jit(solution)/shard_map/psum | solution.py:79
  260.2 0.9 convert_add_fusion.1
  261.1 0.9 fusion.45
  262.0 11.7 %cholesky.44 = f32[128,128]{1,0:T(8,128)S(1)} custom-call(f32[128,128]{1,0:T(8,128)S(1)} %fusion.45), custom_call_target="Cholesky" | custom-call | tf_op jit(solution)/shard_map/jit(cholesky)/cholesky | solution.py:80
  273.8 0.6 compare_reduce_fusion.1
  274.4 0.7 fusion.32
  275.1 9.8 %custom-call.22 = f32[1,128,128]{1,2,0:T(8,128)S(1)} custom-call(f32[1,128,128]{2,1,0:T(8,128)S(1)} %fusion.32), custom_call_target="InvertDiagBlocksLowerTriangular" | custom-call | tf_op jit(solution)/shard_map/jit(_cho_solve)/triangular_solve | solution.py:81
  284.9 0.2 fusion.41
  285.1 0.2 fusion.25
  285.3 59.9 %all-gather.1 = bf16[256,4,128]{2,1,0:T(4,128)(2,1)S(1)} all-gather(bf16[1,4,128]{2,1,0:T(4,128)(2,1)S(1)} %fusion.25), channel_id=1, replica_groups=mesh['gx'=8,'gy'=32] {'gx','gy'}, dimensions={0}, use_global_device_ids=true | all-gather | bytes 263168 | tf_op jit(solution)/shard_map/all_gather | solution.py:92
  345.5 0.2 fusion.28
  345.8 0.2 dynamic-update-slice.2
  346.0 76.5 %all-reduce = bf16[1024]{0:T(1024)(128)(2,1)S(1)} all-reduce(bf16[1024]{0:T(1024)(128)(2,1)S(1)} %dynamic-update-slice.2), channel_id=1, replica_groups=mesh['gx'=8,'gy'=32] {'gx','gy'}, use_global_device_ids=true, to_apply=%add | all-reduce | flops 1024 | bytes 4096
  422.7 34.6 %while.26 = (s32[]{:T(128)}, f32[2,2048]{1,0:T(2,128)S(1)}, f32[2,2048,128]{2,1,0:T(8,128)S(1)}, bf16[2,2048,128]{2,1,0:T(8,128)(2,1)}, bf16[1024,128]{1,0:T(8,1...) while((s32[]{:T(128)}, f32[2,2048]{1,0:T(2,128)S(1)}, ...), condition=%wide.region_5.9_spmd.clone, body=%wide.region_4.8_spmd.clone.sunk | while | flops 1157627904 | bytes 14736005 | solution.py:38
  422.7 14.7 %fusion.135 = bf16[2048,1024]{1,0:T(8,128)(2,1)S(1)} fusion(bf16[1024,128]{1,0:T(8,128)(2,1)S(1)} %get-tuple-element.386, s32[1024]{0:T(1024)S(1)} %get-tuple-element.391, s32[2048]{0:T(1024)S(1)} %get-tuple-element.392, s32[1024]{0:T(1024)S(1)} %get-tuple-element.389, s32[2048]{0:T(1024)S(1)} %get-tuple-element.390, ...), kind=kOutput, calls=%fused_computation.10.clone.1 | convolution fusion | flops 616562688 | bytes 5005824 | tf_op jit(solution)/shard_map/while/body/eval_jaxpr/dot_general | solution.py:30
  437.5 1.3 fusion.137
  438.7 1.2 fusion.136
  440.0 14.7 %fusion.135 = bf16[2048,1024]{1,0:T(8,128)(2,1)S(1)} fusion(bf16[1024,128]{1,0:T(8,128)(2,1)S(1)} %get-tuple-element.386, s32[1024]{0:T(1024)S(1)} %get-tuple-element.391, s32[2048]{0:T(1024)S(1)} %get-tuple-element.392, s32[1024]{0:T(1024)S(1)} %get-tuple-element.389, s32[2048]{0:T(1024)S(1)} %get-tuple-element.390, ...), kind=kOutput, calls=%fused_computation.10.clone.1 | convolution fusion | flops 616562688 | bytes 5005824 | tf_op jit(solution)/shard_map/while/body/eval_jaxpr/dot_general | solution.py:30
  454.7 1.3 fusion.137
  456.0 1.2 fusion.136
  457.4 1.5 subtract_convert_fusion.1
  458.9 0.6 gather_fusion.2
  459.5 1.0 fusion.85
  460.6 0.6 gather_fusion.3
  461.2 62.8 %all-gather.2 = bf16[256,4,128]{2,1,0:T(4,128)(2,1)} all-gather(bf16[1,4,128]{2,1,0:T(4,128)(2,1)S(1)} %bitcast.217), channel_id=1, replica_groups=mesh['gx'=8,'gy'=32] {'gx','gy'}, dimensions={0}, use_global_device_ids=true | all-gather | bytes 263168 | tf_op jit(solution)/shard_map/all_gather | solution.py:91
  524.2 77.2 %psum.31 = f32[128]{0:T(128)S(1)} all-reduce(f32[128]{0:T(128)S(1)} %convolution_bitcast_fusion.5), channel_id=1, replica_groups=mesh['gx'=8,'gy'=32] {'gx','gy'}, use_global_device_ids=true, to_apply=%region_7.11 | all-reduce | flops 128 | bytes 1024 | tf_op jit(solution)/shard_map/psum | solution.py:79
  601.5 95.7 %all-reduce.7.cloned.1.call-done = f32[128,128]{0,1:T(8,128)} async-done(((f32[128,128]{0,1:T(8,128)}), f32[128,128]{0,1:T(8,128)}) %all-reduce.7.cloned.1.call-update) | async-done | bytes 65552 | tf_op jit(solution)/shard_map/psum | solution.py:79
  697.2 0.9 convert_add_fusion
  698.1 0.9 fusion.39
  699.0 11.7 %cholesky.55 = f32[128,128]{1,0:T(8,128)S(1)} custom-call(f32[128,128]{1,0:T(8,128)S(1)} %fusion.39), custom_call_target="Cholesky" | custom-call | tf_op jit(solution)/shard_map/jit(cholesky)/cholesky | solution.py:80
  710.7 0.6 compare_reduce_fusion
  711.4 0.7 fusion.33
  712.0 9.8 %custom-call.24 = f32[1,128,128]{1,2,0:T(8,128)S(1)} custom-call(f32[1,128,128]{2,1,0:T(8,128)S(1)} %fusion.33), custom_call_target="InvertDiagBlocksLowerTriangular" | custom-call | tf_op jit(solution)/shard_map/jit(_cho_solve)/triangular_solve | solution.py:81
  721.8 0.2 fusion.35
  722.0 0.2 fusion.24
  722.2 59.9 %all-gather.3 = bf16[256,4,128]{2,1,0:T(4,128)(2,1)S(1)} all-gather(bf16[1,4,128]{2,1,0:T(4,128)(2,1)S(1)} %fusion.24), channel_id=1, replica_groups=mesh['gx'=8,'gy'=32] {'gx','gy'}, dimensions={0}, use_global_device_ids=true | all-gather | bytes 263168 | tf_op jit(solution)/shard_map/all_gather | solution.py:92
  782.5 0.2 fusion.31
  782.8 0.2 dynamic-update-slice.3
  783.0 76.6 %all-reduce.1 = bf16[1024]{0:T(1024)(128)(2,1)S(1)} all-reduce(bf16[1024]{0:T(1024)(128)(2,1)S(1)} %dynamic-update-slice.3), channel_id=1, replica_groups=mesh['gx'=8,'gy'=32] {'gx','gy'}, use_global_device_ids=true, to_apply=%add.1 | all-reduce | flops 1024 | bytes 4096
  859.8 35.3 %while.27 = (s32[]{:T(128)}, f32[2,2048]{1,0:T(2,128)S(1)}, f32[2,2048,128]{2,1,0:T(8,128)S(1)}, bf16[2,2048,128]{2,1,0:T(8,128)(2,1)S(1)}, bf16[1024,128]{1,0:T...) while((s32[]{:T(128)}, f32[2,2048]{1,0:T(2,128)S(1)}, ...), condition=%wide.region_9.13_spmd.clone, body=%wide.region_8.12_spmd.clone.sunk | while | flops 1157627904 | bytes 14735497 | solution.py:38
  859.8 15.1 %fusion.144 = bf16[2048,1024]{1,0:T(8,128)(2,1)S(1)} fusion(bf16[1024,128]{1,0:T(8,128)(2,1)} %get-tuple-element.425, s32[1024]{0:T(1024)S(1)} %get-tuple-element.430, s32[2048]{0:T(1024)S(1)} %get-tuple-element.431, s32[1024]{0:T(1024)S(1)} %get-tuple-element.428, s32[2048]{0:T(1024)S(1)} %get-tuple-element.429, ...), kind=kOutput, calls=%fused_computation.24.clone.1 | convolution fusion | flops 616562688 | bytes 5005316 | tf_op jit(solution)/shard_map/while/body/eval_jaxpr/dot_general | solution.py:30
  874.9 1.3 fusion.146
  876.2 1.2 fusion.145
  877.5 15.1 %fusion.144 = bf16[2048,1024]{1,0:T(8,128)(2,1)S(1)} fusion(bf16[1024,128]{1,0:T(8,128)(2,1)} %get-tuple-element.425, s32[1024]{0:T(1024)S(1)} %get-tuple-element.430, s32[2048]{0:T(1024)S(1)} %get-tuple-element.431, s32[1024]{0:T(1024)S(1)} %get-tuple-element.428, s32[2048]{0:T(1024)S(1)} %get-tuple-element.429, ...), kind=kOutput, calls=%fused_computation.24.clone.1 | convolution fusion | flops 616562688 | bytes 5005316 | tf_op jit(solution)/shard_map/while/body/eval_jaxpr/dot_general | solution.py:30
  892.5 1.3 fusion.146
  893.8 1.2 fusion.145
  895.1 1.2 subtract_convert_fusion
  896.4 0.6 copy.37
  (72 shorter events, 4.1 us)
Async XLA Ops:
  7.2 253.0 %all-reduce.5.cloned.1.call-start = ((), (), s32[]{:S(2)}) async-start(), calls=%async_computation | async-start | bytes 131072 | tf_op jit(solution)/shard_map/psum | solution.py:79
  13.0 684.2 %all-reduce.7.cloned.1.call-start = ((), (), s32[]{:S(2)}) async-start(), calls=%async_computation.1 | async-start | bytes 131072 | tf_op jit(solution)/shard_map/psum | solution.py:79
  84.2 338.5 %copy-start.9 = (f32[4]{0:T(128)}, f32[4]{0:T(128)S(1)}, u32[]{:S(2)}) copy-start(f32[4]{0:T(128)S(1)} %get-tuple-element.152) | copy-start | bytes 52
  457.3 1.6 copy-start.3
  457.3 2.2 copy-start.7
  457.3 3.2 copy-start.2
  457.3 66.7 %copy-start.8 = (f32[4]{0:T(128)S(1)}, f32[4]{0:T(128)}, u32[]{:S(2)}) copy-start(f32[4]{0:T(128)} %fusion.62) | copy-start | bytes 52
  457.4 66.7 %copy-start.10 = (f32[4]{0:T(128)S(1)}, f32[4]{0:T(128)}, u32[]{:S(2)}) copy-start(f32[4]{0:T(128)} %copy-done.9) | copy-start | bytes 52
  457.4 264.7 %copy-start.6 = (f32[4]{0:T(128)S(1)}, f32[4]{0:T(128)}, u32[]{:S(2)}) copy-start(f32[4]{0:T(128)} %get-tuple-element.151) | copy-start | bytes 52
  457.4 402.4 %copy-start.4 = (s32[1024]{0:T(1024)S(1)}, s32[1024]{0:T(1024)}, u32[]{:S(2)}) copy-start(s32[1024]{0:T(1024)} %get-tuple-element.404) | copy-start | bytes 12292
  457.4 402.4 %copy-start.5 = (s32[1024]{0:T(1024)S(1)}, s32[1024]{0:T(1024)}, u32[]{:S(2)}) copy-start(s32[1024]{0:T(1024)} %get-tuple-element.402) | copy-start | bytes 12292
  460.6 399.2 %copy-start = (f32[2,2048]{1,0:T(2,128)}, f32[2,2048]{1,0:T(2,128)S(1)}, u32[]{:S(2)}) copy-start(f32[2,2048]{1,0:T(2,128)S(1)} %fusion.83) | copy-start | bytes 49156
  895.1 1.3 copy-start.1
Sparse Core Ops, SparseCore 0:
  14.1 246.0 all-reduce.4
  460.6 236.4 all-reduce.6
where the time goes:
time: 906 us; the launch traced here: 904 us
  blocking collectives  555 us (61%)
  waiting for transfers between devices  194 us (21%)
  matrix products  73.8 us (8%)
  other arithmetic  54.9 us (6%)
  between operations  14.4 us (2%)
  local copies, waits for them, and re-layouts  11.7 us (1%)
    psum x2, waiting for transfers between devices, body(): gram_all, proj_all = lax.psum((gram_term, proj_term), ('gx', 'gy'))  194 us
    unnamed x2, blocking collectives  153 us
    psum x2, blocking collectives, body(): gram_all, proj_all = lax.psum((gram_term, proj_term), ('gx', 'gy'))  153 us
    all_gather x2, blocking collectives, body(): lax.all_gather(panel_zb, ('gx', 'gy'), axis=0, tiled=True)  130 us
    all_gather x2, blocking collectives, body(): lax.all_gather(panel_qb, ('gx', 'gy'), axis=0, tiled=True)  120 us
    dot_general x4, matrix products, per_level(): jnp.dot(spread_lev, panel_zb.T, preferred_element_type=jnp.float32)  59.5 us
    another operation x6, other arithmetic, body(): factor = jnp.linalg.cholesky(identity + gram_all)  24.8 us
    another operation x4, other arithmetic, body(): ens_weights = jax.scipy.linalg.cho_solve((factor, True), proj_all)  20.9 us
  transfers between devices with their start and end apart: 2, of which 2 were waited for; matrix products, arithmetic and copies ran while one was open for 1% of the time, Pallas kernels for 0%

commit v1 on v0

--- a/solution.py
+++ b/solution.py
@@ -4,6 +4,11 @@
 from jax.sharding import PartitionSpec as P
 
 PRECISE = lax.Precision.HIGHEST
+
+
+def axis_by_axis(x, inner_axis, outer_axis):
+    inner = lax.psum(x, inner_axis)
+    return lax.psum(inner, outer_axis)
 
 
 def taper(dist_sq, radius):
@@ -76,7 +81,7 @@
         ).reshape(-1)
         gram_term = jnp.dot(weighted.T, weighted, precision=PRECISE)
         proj_term = jnp.dot(weighted.T, innov_norm, precision=PRECISE)
-        gram_all, proj_all = lax.psum((gram_term, proj_term), ("gx", "gy"))
+        gram_all, proj_all = axis_by_axis((gram_term, proj_term), "gy", "gx")
         factor = jnp.linalg.cholesky(identity + gram_all)
         ens_weights = jax.scipy.linalg.cho_solve((factor, True), proj_all)
         panel_e = (innov_norm - jnp.dot(weighted, ens_weights, precision=PRECISE)) / obs_sd

time: 906 us -> 874 us (0.965)
  waiting for transfers between devices: 194 us -> 137 us
  blocking collectives: 555 us -> 580 us
    psum x2 -> x4, waiting for transfers between devices: 194 us -> 137 us  [the longest x2 137 us: axis_by_axis(): inner = lax.psum(x, inner_axis)]
    psum x2 -> x4, blocking collectives: 153 us -> 179 us  [the longest x2 118 us: axis_by_axis(): inner = lax.psum(x, inner_axis)]
  transfers between devices with their start and end apart: 2 -> 4, of which waited for: 2 -> 2; matrix products, arithmetic and copies ran while one was open for 1% -> 1% of each run, Pallas kernels for 0% -> 0%
where the time goes in v1:
time: 874 us; the launch traced here: 872 us
  blocking collectives  580 us (66%)
  waiting for transfers between devices  137 us (16%)
  matrix products  73.7 us (8%)
  other arithmetic  55 us (6%)
  between operations  14.1 us (2%)
  local copies, waits for them, and re-layouts  11.8 us (1%)
    unnamed x2, blocking collectives  155 us
    psum x2, waiting for transfers between devices, axis_by_axis(): inner = lax.psum(x, inner_axis)  137 us
    all_gather x2, blocking collectives, body(): lax.all_gather(panel_zb, ('gx', 'gy'), axis=0, tiled=True)  130 us
    psum x2, blocking collectives, axis_by_axis(): inner = lax.psum(x, inner_axis)  118 us
    all_gather x2, blocking collectives, body(): lax.all_gather(panel_qb, ('gx', 'gy'), axis=0, tiled=True)  116 us
    psum x2, blocking collectives, axis_by_axis(): return lax.psum(inner, outer_axis)  61.6 us
    dot_general x4, matrix products, per_level(): jnp.dot(spread_lev, panel_zb.T, preferred_element_type=jnp.float32)  59.5 us
    another operation x6, other arithmetic, body(): factor = jnp.linalg.cholesky(identity + gram_all)  24.8 us
  transfers between devices with their start and end apart: 4, of which 2 were waited for; matrix products, arithmetic and copies ran while one was open for 1% of the time, Pallas kernels for 0%

profile of v1, /device:TPU:1, one launch (start us, length us, event | category | flops | bytes accessed | tf_op | source)
XLA Modules:
  0.0 872.4 jit_solution(8183141982680188306)
XLA Ops:
  7.2 0.7 fusion.89
  8.0 0.7 fusion.90
  8.7 0.7 fusion.88
  9.4 0.7 fusion.87
  10.6 1.4 gather_fusion
  12.0 1.0 fusion.84
  13.3 0.7 copy.38
  14.0 0.6 gather_fusion.1
  14.7 0.7 fusion.86
  15.4 66.7 %all-gather = bf16[256,4,128]{2,1,0:T(4,128)(2,1)S(1)} all-gather(bf16[1,4,128]{2,1,0:T(4,128)(2,1)S(1)} %bitcast.216), channel_id=1, replica_groups=mesh['gx'=8,'gy'=32] {'gx','gy'}, dimensions={0}, use_global_device_ids=true | all-gather | bytes 263168 | tf_op jit(solution)/shard_map/all_gather | solution.py:96
  83.5 0.8 multiply_reduce_fusion
  84.3 0.5 broadcast_multiply_fusion
  84.8 0.6 fusion.81
  85.4 0.6 fusion.91
  86.2 67.9 %all-reduce.7.cloned.1.call-done = f32[128,128]{0,1:T(8,128)} async-done(((f32[128,128]{0,1:T(8,128)}), f32[128,128]{0,1:T(8,128)}) %all-reduce.7.cloned.1.call-update) | async-done | bytes 65552 | tf_op jit(solution)/shard_map/psum | solution.py:10
  154.2 0.8 fusion.62
  154.9 58.8 %psum.58 = f32[128]{0:T(128)S(1)} all-reduce(f32[128]{0:T(128)S(1)} %convolution_bitcast_fusion.9), channel_id=1, replica_groups=mesh['gx'=8,'gy'=32] {'gy'}, use_global_device_ids=true, to_apply=%region_4.6 | all-reduce | flops 128 | bytes 1024 | tf_op jit(solution)/shard_map/psum | solution.py:10
  213.8 30.7 %psum.59 = f32[128]{0:T(128)S(1)} all-reduce(f32[128]{0:T(128)S(1)} %psum.58), channel_id=1, replica_groups=mesh['gx'=8,'gy'=32] {'gx'}, use_global_device_ids=true, to_apply=%region_5.7 | all-reduce | flops 128 | bytes 1024 | tf_op jit(solution)/shard_map/psum | solution.py:11
  244.5 0.9 convert_add_fusion.1
  245.5 0.9 fusion.45
  246.3 11.7 %cholesky.44 = f32[128,128]{1,0:T(8,128)S(1)} custom-call(f32[128,128]{1,0:T(8,128)S(1)} %fusion.45), custom_call_target="Cholesky" | custom-call | tf_op jit(solution)/shard_map/jit(cholesky)/cholesky | solution.py:85
  258.1 0.6 compare_reduce_fusion.1
  258.7 0.7 fusion.32
  259.4 9.8 %custom-call.22 = f32[1,128,128]{1,2,0:T(8,128)S(1)} custom-call(f32[1,128,128]{2,1,0:T(8,128)S(1)} %fusion.32), custom_call_target="InvertDiagBlocksLowerTriangular" | custom-call | tf_op jit(solution)/shard_map/jit(_cho_solve)/triangular_solve | solution.py:86
  269.2 0.2 fusion.41
  269.6 57.9 %all-gather.1 = bf16[256,4,128]{2,1,0:T(4,128)(2,1)S(1)} all-gather(bf16[1,4,128]{2,1,0:T(4,128)(2,1)S(1)} %fusion.25), channel_id=1, replica_groups=mesh['gx'=8,'gy'=32] {'gx','gy'}, dimensions={0}, use_global_device_ids=true | all-gather | bytes 263168 | tf_op jit(solution)/shard_map/all_gather | solution.py:97
  327.8 0.2 fusion.28
  328.1 0.2 dynamic-update-slice.2
  328.3 77.4 %all-reduce = bf16[1024]{0:T(1024)(128)(2,1)S(1)} all-reduce(bf16[1024]{0:T(1024)(128)(2,1)S(1)} %dynamic-update-slice.2), channel_id=1, replica_groups=mesh['gx'=8,'gy'=32] {'gx','gy'}, use_global_device_ids=true, to_apply=%add | all-reduce | flops 1024 | bytes 4096
  405.9 34.6 %while.26 = (s32[]{:T(128)}, f32[2,2048]{1,0:T(2,128)S(1)}, f32[2,2048,128]{2,1,0:T(8,128)S(1)}, bf16[2,2048,128]{2,1,0:T(8,128)(2,1)}, bf16[1024,128]{1,0:T(8,1...) while((s32[]{:T(128)}, f32[2,2048]{1,0:T(2,128)S(1)}, ...), condition=%wide.region_7.11_spmd.clone, body=%wide.region_6.10_spmd.clone.sunk | while | flops 1157627904 | bytes 14736005 | solution.py:43
  405.9 14.7 %fusion.135 = bf16[2048,1024]{1,0:T(8,128)(2,1)S(1)} fusion(bf16[1024,128]{1,0:T(8,128)(2,1)S(1)} %get-tuple-element.386, s32[1024]{0:T(1024)S(1)} %get-tuple-element.391, s32[2048]{0:T(1024)S(1)} %get-tuple-element.392, s32[1024]{0:T(1024)S(1)} %get-tuple-element.389, s32[2048]{0:T(1024)S(1)} %get-tuple-element.390, ...), kind=kOutput, calls=%fused_computation.10.clone.1 | convolution fusion | flops 616562688 | bytes 5005824 | tf_op jit(solution)/shard_map/while/body/eval_jaxpr/dot_general | solution.py:35
  420.6 1.3 fusion.137
  421.9 1.2 fusion.136
  423.2 14.7 %fusion.135 = bf16[2048,1024]{1,0:T(8,128)(2,1)S(1)} fusion(bf16[1024,128]{1,0:T(8,128)(2,1)S(1)} %get-tuple-element.386, s32[1024]{0:T(1024)S(1)} %get-tuple-element.391, s32[2048]{0:T(1024)S(1)} %get-tuple-element.392, s32[1024]{0:T(1024)S(1)} %get-tuple-element.389, s32[2048]{0:T(1024)S(1)} %get-tuple-element.390, ...), kind=kOutput, calls=%fused_computation.10.clone.1 | convolution fusion | flops 616562688 | bytes 5005824 | tf_op jit(solution)/shard_map/while/body/eval_jaxpr/dot_general | solution.py:35
  437.9 1.3 fusion.137
  439.2 1.2 fusion.136
  440.5 1.5 subtract_convert_fusion.1
  442.1 0.6 gather_fusion.2
  442.6 1.0 fusion.85
  443.8 0.6 gather_fusion.3
  444.4 63.2 %all-gather.2 = bf16[256,4,128]{2,1,0:T(4,128)(2,1)} all-gather(bf16[1,4,128]{2,1,0:T(4,128)(2,1)S(1)} %bitcast.217), channel_id=1, replica_groups=mesh['gx'=8,'gy'=32] {'gx','gy'}, dimensions={0}, use_global_device_ids=true | all-gather | bytes 263168 | tf_op jit(solution)/shard_map/all_gather | solution.py:96
  507.6 69.5 %all-reduce.11.cloned.1.call-done = f32[128,128]{0,1:T(8,128)} async-done(((f32[128,128]{0,1:T(8,128)}), f32[128,128]{0,1:T(8,128)}) %all-reduce.11.cloned.1.call-update) | async-done | bytes 65552 | tf_op jit(solution)/shard_map/psum | solution.py:10
  577.3 58.9 %psum.62 = f32[128]{0:T(128)S(1)} all-reduce(f32[128]{0:T(128)S(1)} %convolution_bitcast_fusion.5), channel_id=1, replica_groups=mesh['gx'=8,'gy'=32] {'gy'}, use_global_device_ids=true, to_apply=%region_10.14 | all-reduce | flops 128 | bytes 1024 | tf_op jit(solution)/shard_map/psum | solution.py:10
  636.2 30.9 %psum.63 = f32[128]{0:T(128)S(1)} all-reduce(f32[128]{0:T(128)S(1)} %psum.62), channel_id=1, replica_groups=mesh['gx'=8,'gy'=32] {'gx'}, use_global_device_ids=true, to_apply=%region_11.15 | all-reduce | flops 128 | bytes 1024 | tf_op jit(solution)/shard_map/psum | solution.py:11
  667.1 0.9 convert_add_fusion
  668.1 0.9 fusion.39
  669.0 11.7 %cholesky.55 = f32[128,128]{1,0:T(8,128)S(1)} custom-call(f32[128,128]{1,0:T(8,128)S(1)} %fusion.39), custom_call_target="Cholesky" | custom-call | tf_op jit(solution)/shard_map/jit(cholesky)/cholesky | solution.py:85
  680.7 0.6 compare_reduce_fusion
  681.4 0.7 fusion.33
  682.0 9.8 %custom-call.24 = f32[1,128,128]{1,2,0:T(8,128)S(1)} custom-call(f32[1,128,128]{2,1,0:T(8,128)S(1)} %fusion.33), custom_call_target="InvertDiagBlocksLowerTriangular" | custom-call | tf_op jit(solution)/shard_map/jit(_cho_solve)/triangular_solve | solution.py:86
  691.8 0.2 fusion.35
  692.2 57.9 %all-gather.3 = bf16[256,4,128]{2,1,0:T(4,128)(2,1)S(1)} all-gather(bf16[1,4,128]{2,1,0:T(4,128)(2,1)S(1)} %fusion.24), channel_id=1, replica_groups=mesh['gx'=8,'gy'=32] {'gx','gy'}, dimensions={0}, use_global_device_ids=true | all-gather | bytes 263168 | tf_op jit(solution)/shard_map/all_gather | solution.py:97
  750.5 0.2 fusion.31
  750.7 0.2 dynamic-update-slice.3
  750.9 77.5 %all-reduce.1 = bf16[1024]{0:T(1024)(128)(2,1)S(1)} all-reduce(bf16[1024]{0:T(1024)(128)(2,1)S(1)} %dynamic-update-slice.3), channel_id=1, replica_groups=mesh['gx'=8,'gy'=32] {'gx','gy'}, use_global_device_ids=true, to_apply=%add.1 | all-reduce | flops 1024 | bytes 4096
  828.6 35.3 %while.27 = (s32[]{:T(128)}, f32[2,2048]{1,0:T(2,128)S(1)}, f32[2,2048,128]{2,1,0:T(8,128)S(1)}, bf16[2,2048,128]{2,1,0:T(8,128)(2,1)S(1)}, bf16[1024,128]{1,0:T...) while((s32[]{:T(128)}, f32[2,2048]{1,0:T(2,128)S(1)}, ...), condition=%wide.region_13.17_spmd.clone, body=%wide.region_12.16_spmd.clone.sunk | while | flops 1157627904 | bytes 14735497 | solution.py:43
  828.6 15.1 %fusion.144 = bf16[2048,1024]{1,0:T(8,128)(2,1)S(1)} fusion(bf16[1024,128]{1,0:T(8,128)(2,1)} %get-tuple-element.425, s32[1024]{0:T(1024)S(1)} %get-tuple-element.430, s32[2048]{0:T(1024)S(1)} %get-tuple-element.431, s32[1024]{0:T(1024)S(1)} %get-tuple-element.428, s32[2048]{0:T(1024)S(1)} %get-tuple-element.429, ...), kind=kOutput, calls=%fused_computation.24.clone.1 | convolution fusion | flops 616562688 | bytes 5005316 | tf_op jit(solution)/shard_map/while/body/eval_jaxpr/dot_general | solution.py:35
  843.7 1.3 fusion.146
  845.0 1.2 fusion.145
  846.3 15.1 %fusion.144 = bf16[2048,1024]{1,0:T(8,128)(2,1)S(1)} fusion(bf16[1024,128]{1,0:T(8,128)(2,1)} %get-tuple-element.425, s32[1024]{0:T(1024)S(1)} %get-tuple-element.430, s32[2048]{0:T(1024)S(1)} %get-tuple-element.431, s32[1024]{0:T(1024)S(1)} %get-tuple-element.428, s32[2048]{0:T(1024)S(1)} %get-tuple-element.429, ...), kind=kOutput, calls=%fused_computation.24.clone.1 | convolution fusion | flops 616562688 | bytes 5005316 | tf_op jit(solution)/shard_map/while/body/eval_jaxpr/dot_general | solution.py:35
  861.4 1.3 fusion.146
  862.7 1.2 fusion.145
  864.0 1.2 subtract_convert_fusion
  865.2 0.6 copy.37
  (80 shorter events, 4.7 us)
Async XLA Ops:
  7.2 146.9 %all-reduce.7.cloned.1.call-start = ((), (), s32[]{:S(2)}) async-start(), calls=%async_computation | async-start | bytes 131072 | tf_op jit(solution)/shard_map/psum | solution.py:10
  13.0 231.5 %all-reduce.9.cloned.1.call-start = ((), (), s32[]{:S(2)}) async-start(), calls=%async_computation.1 | async-start | bytes 131072 | tf_op jit(solution)/shard_map/psum | solution.py:11
  84.3 321.6 %copy-start.9 = (f32[4]{0:T(128)}, f32[4]{0:T(128)S(1)}, u32[]{:S(2)}) copy-start(f32[4]{0:T(128)S(1)} %get-tuple-element.152) | copy-start | bytes 52
  154.1 423.0 %all-reduce.11.cloned.1.call-start = ((), (), s32[]{:S(2)}) async-start(), calls=%async_computation.2 | async-start | bytes 131072 | tf_op jit(solution)/shard_map/psum | solution.py:10
  440.5 1.6 copy-start.3
  440.5 2.2 copy-start.7
  440.5 3.2 copy-start.2
  440.5 136.6 %copy-start.8 = (f32[4]{0:T(128)S(1)}, f32[4]{0:T(128)}, u32[]{:S(2)}) copy-start(f32[4]{0:T(128)} %fusion.62) | copy-start | bytes 52
  440.5 136.6 %copy-start.10 = (f32[4]{0:T(128)S(1)}, f32[4]{0:T(128)}, u32[]{:S(2)}) copy-start(f32[4]{0:T(128)} %copy-done.9) | copy-start | bytes 52
  440.5 251.5 %copy-start.6 = (f32[4]{0:T(128)S(1)}, f32[4]{0:T(128)}, u32[]{:S(2)}) copy-start(f32[4]{0:T(128)} %get-tuple-element.151) | copy-start | bytes 52
  440.5 388.1 %copy-start.4 = (s32[1024]{0:T(1024)S(1)}, s32[1024]{0:T(1024)}, u32[]{:S(2)}) copy-start(s32[1024]{0:T(1024)} %get-tuple-element.404) | copy-start | bytes 12292
  440.5 388.1 %copy-start.5 = (s32[1024]{0:T(1024)S(1)}, s32[1024]{0:T(1024)}, u32[]{:S(2)}) copy-start(s32[1024]{0:T(1024)} %get-tuple-element.402) | copy-start | bytes 12292
  443.7 223.5 %all-reduce.13.cloned.1.call-start = ((), (), s32[]{:S(2)}) async-start(), calls=%async_computation.3 | async-start | bytes 131072 | tf_op jit(solution)/shard_map/psum | solution.py:11
  443.8 384.9 %copy-start = (f32[2,2048]{1,0:T(2,128)}, f32[2,2048]{1,0:T(2,128)S(1)}, u32[]{:S(2)}) copy-start(f32[2,2048]{1,0:T(2,128)S(1)} %fusion.83) | copy-start | bytes 49156
  863.9 1.3 copy-start.1
Sparse Core Ops, SparseCore 0:
  13.1 140.9 all-reduce.6
  156.4 65.5 all-reduce.8
  443.8 133.2 all-reduce.10
  579.3 65.3 all-reduce.12
